TPU v7x, 32 devices: a whole 2x2x4 slice. The times are simulated.
32 devices in a mesh: groups: 2 (over x), wide: 16 (over z, y, core).
Axes of the slice: x: 2, y: 2, z: 4, core: 2. Of those that a mesh axis runs over, the one named last changes fastest.
Arguments:
- queries: bfloat16 [32, 16, 8, 128], P(('groups', 'wide')), parts along dimension 0, may hold values from -250 to 250
- keys_cache: bfloat16 [32, 16, 320, 128], P(('groups', 'wide')), parts along dimension 0, may hold values from -6 to 6
- values_cache: bfloat16 [32, 16, 320, 128], P(('groups', 'wide')), parts along dimension 0, may hold values from -6 to 6
- new_keys: bfloat16 [32, 16, 128], P(('groups', 'wide')), parts along dimension 0, may hold values from -6 to 6
- new_values: bfloat16 [32, 16, 128], P(('groups', 'wide')), parts along dimension 0, may hold values from -6 to 6
- lengths: int32 [64], P('groups'), parts along dimension 0, may hold values from 1 to 320, as said below
- assignment: int32 [64], P('groups'), parts along dimension 0, may hold values from 0 to 31, each once
- residual: bfloat16 [64, 8192], P('groups', 'wide'), parts along dimension 0, may hold values from -6 to 6
- w_out: bfloat16 [8192, 8192], P('wide'), may hold values from -0.0625 to 0.0625
- w_gate: bfloat16 [20480, 8192], P('wide'), may hold values from -0.0625 to 0.0625
- w_up: bfloat16 [20480, 8192], P('wide'), may hold values from -0.0625 to 0.0625
- w_down: bfloat16 [20480, 8192], P('wide'), may hold values from -0.0625 to 0.0625
- norm_gain: float32 [8192], P('wide'), may hold values from 0.25 to 1.75
Outputs:
- mixed: bfloat16 [64, 8192], P('groups', 'wide'), parts along dimension 0
There are 2 independent parts, one for each index of `groups`. A program takes and returns all parts, laid end to end along the dimension named above; an argument that names none is the same for every part. Nothing has to cross between parts.
Inputs may be any that keep to these rules, and one draw needn't show every extreme that they name: `lengths`: every length is at least 1; one cache row has length exactly 320 in every draw. `assignment`: A permutation of the request numbers.
All inputs are finite; a program needn't handle non-finite values.
Results may differ from a plain program's by a relative error of at most 0.0052.
Values may be sent and summed in bfloat16 or wider, within the bound.
No kernel may reach another device: no remote copies, remote signals or barrier semaphores. Data moves between devices by JAX's collectives and lax.ppermute only.
A program may use at most 128 MiB of HBM per device.

v0:
```python
import math

import jax
import jax.numpy as jnp
from jax import lax
from jax.sharding import PartitionSpec as P

D = 8192
KV = 8


KEY_BLOCK = 64
EPSILON = 1e-05
NEG_FILL = -1e30


def contract_last(left, right):
    return lax.dot_general(
        left, right, (((1,), (1,)), ((), ())), preferred_element_type=jnp.float32
    )


def masked_scores(query_rows, keys_local, lens_local, block_index, inv_scale):
    key_block = lax.dynamic_slice_in_dim(keys_local, block_index * KEY_BLOCK, KEY_BLOCK, 1)
    scores = (
        jnp.einsum("rqe,rpe->rqp", query_rows, key_block, preferred_element_type=jnp.float32)
        * inv_scale
    )
    position = block_index * KEY_BLOCK + lax.broadcasted_iota(jnp.int32, scores.shape, 2)
    return jnp.where(position < lens_local[:, None, None], scores, NEG_FILL)


def on_device(
    queries,
    keys_cache,
    values_cache,
    new_keys,
    new_values,
    lengths,
    assignment,
    residual,
    w_out,
    w_gate,
    w_up,
    w_down,
    norm_gain,
):
    my_index = lax.axis_index("wide")
    my_shard = my_index // KV
    req_dev = queries.shape[1]
    query_rows = queries[0]
    keys_local = keys_cache[0]
    values_local = values_cache[0]
    lens_local = lax.dynamic_slice_in_dim(lengths, my_shard * req_dev, req_dev)
    inv_scale = 1.0 / math.sqrt(query_rows.shape[2])
    own_score = (
        jnp.einsum("rqe,re->rq", query_rows, new_keys[0], preferred_element_type=jnp.float32)
        * inv_scale
    )
    block_count = (jnp.max(lens_local) + KEY_BLOCK - 1) // KEY_BLOCK

    def find_top(block_index, running):
        return jnp.maximum(
            running,
            jnp.max(
                masked_scores(query_rows, keys_local, lens_local, block_index, inv_scale), axis=2
            ),
        )

    top_score = lax.fori_loop(0, block_count, find_top, own_score)
    own_weight = jnp.exp(own_score - top_score)
    own_low = lax.optimization_barrier(own_weight.astype(jnp.bfloat16)).astype(jnp.float32)
    start_state = (own_weight, own_low[:, :, None] * new_values[0].astype(jnp.float32)[:, None, :])

    def accumulate(block_index, state_pair):
        total_sum, weighted = state_pair
        weights = jnp.exp(
            masked_scores(query_rows, keys_local, lens_local, block_index, inv_scale)
            - top_score[:, :, None]
        )
        value_block = lax.dynamic_slice_in_dim(values_local, block_index * KEY_BLOCK, KEY_BLOCK, 1)
        weighted = weighted + jnp.einsum(
            "rqp,rpe->rqe",
            weights.astype(jnp.bfloat16),
            value_block,
            preferred_element_type=jnp.float32,
        )
        return (total_sum + jnp.sum(weights, axis=2), weighted)

    total_sum, weighted = lax.fori_loop(0, block_count, accumulate, start_state)
    attended = (weighted / total_sum[:, :, None]).astype(jnp.bfloat16).reshape(1, req_dev, -1)
    feat_width = attended.shape[2]
    head_piece = lax.all_gather(attended, "wide", axis=0, tiled=True)

    def one_source(offset, running):
        source_shard = offset // KV
        source_group = offset % KV
        request_ids = lax.dynamic_slice_in_dim(assignment, source_shard * req_dev, req_dev)
        out_cols = lax.dynamic_slice_in_dim(w_out, source_group * feat_width, feat_width, 1)
        source_rows = lax.dynamic_index_in_dim(head_piece, offset, 0, keepdims=False)
        term = contract_last(source_rows, out_cols)
        return running.at[request_ids].add(term)

    projected = lax.fori_loop(
        0,
        head_piece.shape[0],
        one_source,
        jnp.zeros((assignment.shape[0], w_out.shape[0]), jnp.float32),
    )
    hidden_state = residual.astype(jnp.float32) + projected
    row_squares = lax.psum(jnp.sum(hidden_state * hidden_state, axis=1), "wide")
    inv_rms = lax.rsqrt(row_squares / D + EPSILON)
    normed_cols = (hidden_state * inv_rms[:, None] * norm_gain[None, :]).astype(jnp.bfloat16)
    normed_piece = lax.all_gather(normed_cols, "wide", axis=1, tiled=True)
    gate_val = contract_last(normed_piece, w_gate)
    up_val = contract_last(normed_piece, w_up)
    activated = (jax.nn.silu(gate_val) * up_val).astype(jnp.bfloat16)
    down_terms = jnp.dot(activated, w_down, preferred_element_type=jnp.float32)
    down_part = lax.psum_scatter(down_terms, "wide", scatter_dimension=1, tiled=True)
    return (hidden_state + down_part).astype(jnp.bfloat16)


def solution(mesh):
    placed = (
        P(("groups", "wide"), None, None, None),
        P(("groups", "wide"), None, None, None),
        P(("groups", "wide"), None, None, None),
        P(("groups", "wide"), None, None),
        P(("groups", "wide"), None, None),
        P("groups"),
        P("groups"),
        P("groups", "wide"),
        P("wide", None),
        P("wide", None),
        P("wide", None),
        P("wide", None),
        P("wide"),
    )
    return jax.shard_map(
        on_device, mesh=mesh, in_specs=placed, out_specs=P("groups", "wide"), check_vma=False
    )
```

profile of v0, /device:TPU:0, one launch (start us, length us, event | category | flops | bytes accessed | tf_op | source)
XLA Modules:
  0.0 248.6 jit_solution(5730291661640036402)
XLA Ops:
  6.5 1.5 fusion.24
  8.7 0.9 fusion.20
  9.6 6.5 %while.37 = (s32[]{:T(128)}, f32[16,8]{1,0:T(8,128)S(1)}, s32[]{:T(128)}, s32[16]{0:T(128)S(1)}, bf16[16,320,128]{2,1,0:T(8,128)(2,1)}, /*index=5*/bf16[16,8,128...) while((s32[]{:T(128)}, f32[16,8]{1,0:T(8,128)S(1)}, s32[]{:T(128)}, s32[16]{0:T(128)S(1)}, ...), condition=%wide.region_3.4_spmd, body=%wide.region_1.3_spmd.sunk | while | flops 2129990 | bytes 297691 | solution.py:70
  9.6 1.3 fusion.49
  10.9 1.3 fusion.49
  12.2 1.3 fusion.49
  13.5 1.3 fusion.49
  14.8 1.3 fusion.49
  16.9 12.3 %while.38 = (s32[]{:T(128)}, f32[16,8]{1,0:T(8,128)S(1)}, f32[16,8,128]{2,1,0:T(8,128)S(1)}, s32[]{:T(128)}, s32[16]{0:T(128)S(1)}, /*index=5*/bf16[16,320,128]{...) while((s32[]{:T(128)}, f32[16,8]{1,0:T(8,128)S(1)}, ...), condition=%wide.region_6.7_spmd, body=%wide.region_4.6_spmd.sunk | while | flops 4259910 | bytes 724215 | solution.py:90
  17.0 1.3 fusion.53
  18.2 1.1 convolution_add_fusion.2
  19.4 1.3 fusion.53
  20.7 1.1 convolution_add_fusion.2
  21.9 1.3 fusion.53
  23.2 1.1 convolution_add_fusion.2
  24.3 1.3 fusion.53
  25.6 1.1 convolution_add_fusion.2
  26.8 1.3 fusion.53
  28.1 1.1 convolution_add_fusion.2
  29.4 21.5 %all_gather.6 = bf16[16,16,1024]{2,1,0:T(8,128)(2,1)S(1)} all-gather(bf16[1,16,1024]{2,1,0:T(8,128)(2,1)S(1)} %reshape.17), channel_id=1, replica_groups=mesh['groups'=2,'wide'=16] {'wide'}, dimensions={0}, use_global_device_ids=true | all-gather | bytes 557056 | tf_op jit(solution)/shard_map/all_gather | solution.py:93
  50.9 50.0 %while.39 = (s32[]{:T(128)}, f32[32,512]{1,0:T(8,128)S(1)}, s32[32]{0:T(128)}, bf16[16,16,1024]{2,1,0:T(8,128)(2,1)S(1)}, bf16[512,8192]{1,0:T(8,128)(2,1)}, /*i...) while((s32[]{:T(128)}, f32[32,512]{1,0:T(8,128)S(1)}, ...), condition=%wide.region_9.10_spmd, body=%wide.region_7.9_spmd.sunk | while | flops 16785476 | bytes 1212976 | solution.py:104
  51.6 1.6 fusion.56
  53.2 0.8 scatter_fusion
  54.7 1.6 fusion.56
  56.3 0.8 scatter_fusion
  57.1 0.7 compare_select_fusion.2
  57.9 1.6 fusion.56
  59.5 0.8 scatter_fusion
  61.0 1.6 fusion.56
  62.6 0.8 scatter_fusion
  63.4 0.7 compare_select_fusion.2
  64.1 1.6 fusion.56
  65.7 0.8 scatter_fusion
  67.2 1.6 fusion.56
  68.8 0.8 scatter_fusion
  70.4 1.6 fusion.56
  72.0 0.8 scatter_fusion
  73.5 1.6 fusion.56
  75.1 0.8 scatter_fusion
  76.6 1.6 fusion.56
  78.2 0.8 scatter_fusion
  79.7 1.6 fusion.56
  81.3 0.8 scatter_fusion
  82.9 1.6 fusion.56
  84.5 0.8 scatter_fusion
  86.0 1.6 fusion.56
  87.6 0.8 scatter_fusion
  89.1 1.6 fusion.56
  90.7 0.8 scatter_fusion
  92.2 1.6 fusion.56
  93.8 0.8 scatter_fusion
  95.3 1.6 fusion.56
  96.9 0.8 scatter_fusion
  98.5 1.6 fusion.56
  100.1 0.8 scatter_fusion
  100.8 0.9 multiply_reduce_fusion
  101.7 29.8 %psum.7 = f32[32]{0:T(128)S(1)} all-reduce(f32[32]{0:T(128)S(1)} %multiply_reduce_fusion), channel_id=1, replica_groups=mesh['groups'=2,'wide'=16] {'wide'}, use_global_device_ids=true, to_apply=%region_11.12 | all-reduce | flops 32 | bytes 256 | tf_op jit(solution)/shard_map/psum | solution.py:111
  131.6 0.9 multiply_convert_fusion
  132.4 18.8 %all_gather.7 = bf16[32,8192]{1,0:T(8,128)(2,1)S(1)} all-gather(bf16[32,512]{1,0:T(8,128)(2,1)S(1)} %multiply_convert_fusion), channel_id=1, replica_groups=mesh['groups'=2,'wide'=16] {'wide'}, dimensions={1}, use_global_device_ids=true | all-gather | bytes 557056 | tf_op jit(solution)/shard_map/all_gather | solution.py:114
  151.2 10.4 %fusion.26 = f32[32,1280]{1,0:T(8,128)S(1)} fusion(bf16[32,8192]{1,0:T(8,128)(2,1)S(1)} %all_gather.7, bf16[1280,8192]{1,0:T(8,128)(2,1)} %param.28), kind=kOutput, calls=%fused_computation.44 | convolution fusion | flops 671088640 | bytes 21659648 | tf_op jit(solution)/shard_map/dot_general | solution.py:18
  161.6 10.5 %fusion.19 = bf16[32,1280]{1,0:T(8,128)(2,1)S(1)} fusion(bf16[32,8192]{1,0:T(8,128)(2,1)S(1)} %all_gather.7, bf16[1280,8192]{1,0:T(8,128)(2,1)} %param.29, f32[32,1280]{1,0:T(8,128)S(1)} %fusion.26), kind=kOutput, calls=%fused_computation.27 | convolution fusion | flops 671334400 | bytes 21741568 | tf_op jit(solution)/shard_map/dot_general | solution.py:18
  172.1 11.7 %fusion.27 = f32[32,8192]{1,0:T(8,128)} fusion(bf16[32,1280]{1,0:T(8,128)(2,1)S(1)} %fusion.19, bf16[1280,8192]{1,0:T(8,128)(2,1)} %param.30), kind=kOutput, calls=%fused_computation.45 | convolution fusion | flops 671088640 | bytes 22102016 | tf_op jit(solution)/shard_map/dot_general | solution.py:118
  183.9 56.4 %reduce-scatter.2.cloned.1.call-done = f32[32,512]{1,0:T(8,128)} async-done(((f32[32,8192]{1,0:T(8,128)}), f32[32,512]{1,0:T(8,128)}) %reduce-scatter.2.cloned.1.call-update) | async-done | bytes 65552 | tf_op jit(solution)/shard_map/reduce_scatter | solution.py:119
  240.3 1.5 add_convert_fusion
  (51 shorter events, 11.3 us)
Async XLA Ops:
  6.5 2.2 copy-start
  6.5 233.7 %reduce-scatter.2.cloned.1.call-start = ((), (), s32[]{:S(2)}) async-start(), calls=%async_computation.1 | async-start | bytes 1114112 | tf_op jit(solution)/shard_map/reduce_scatter | solution.py:119
  161.6 80.1 %copy-start.1 = (bf16[1,16,128]{2,1,0:T(8,128)(2,1)S(1)}, bf16[1,16,128]{2,1,0:T(8,128)(2,1)}, u32[]{:S(2)}) copy-start(bf16[1,16,128]{2,1,0:T(8,128)(2,1)} %param.22) | copy-start | bytes 12292
  172.1 68.1 %copy-start.2 = (bf16[32,512]{1,0:T(8,128)(2,1)S(1)}, bf16[32,512]{1,0:T(8,128)(2,1)}, u32[]{:S(2)}) copy-start(bf16[32,512]{1,0:T(8,128)(2,1)} %param.26) | copy-start | bytes 98308
Sparse Core Ops, SparseCore 0:
  184.0 56.2 reduce-scatter.1
where the time goes:
time: 250 us; the launch traced here: 249 us
  matrix products  77.6 us (31%)
  blocking collectives  70.1 us (28%)
  waiting for transfers between devices  56.4 us (23%)
  other arithmetic  29.4 us (12%)
  between operations  14.2 us (6%)
    reduce_scatter x1, waiting for transfers between devices, on_device(): lax.psum_scatter(down_terms, 'wide', scatter_dimension=1, tiled=True)  56.4 us
    dot_general x18, matrix products, contract_last(): lax.dot_general(left, right, (((1,), (1,)), ((), ())), preferred_element_...  46.5 us
    psum x1, blocking collectives, on_device(): row_squares = lax.psum(jnp.sum(hidden_state * hidden_state, axis=1), 'wide')  29.8 us
    all_gather x1, blocking collectives, on_device(): head_piece = lax.all_gather(attended, 'wide', axis=0, tiled=True)  21.5 us
    all_gather x1, blocking collectives, on_device(): normed_piece = lax.all_gather(normed_cols, 'wide', axis=1, tiled=True)  18.8 us
    dot_general x10, matrix products, masked_scores(): jnp.einsum('rqe,rpe->rqp', query_rows, key_block, preferred_element_type=...  12.9 us
    scatter-add x16, other arithmetic, one_source(): return running.at[request_ids].add(term)  12 us
    select_n x16, other arithmetic, one_source(): return running.at[request_ids].add(term)  11.7 us
  transfers between devices with their start and end apart: 1, of which 1 were waited for; matrix products, arithmetic and copies ran while one was open for 0% of the time, Pallas kernels for 0%

commit v1 on v0

--- a/solution.py
+++ b/solution.py
@@ -1,23 +1,572 @@
+import functools
 import math
 
 import jax
 import jax.numpy as jnp
 from jax import lax
+from jax.experimental import pallas as pl
+from jax.experimental.pallas import tpu as pltpu
 from jax.sharding import PartitionSpec as P
-
-D = 8192
-KV = 8
-
 
 KEY_BLOCK = 64
 EPSILON = 1e-05
 NEG_FILL = -1e30
+ROWS = 256
+LANES = 128
+CACHE_CUTS = 4
+DOWN_SLOTS = 2
+DOWN_AHEAD = 2
+
+
+HBM = pl.BlockSpec(memory_space=pltpu.HBM)
+VMEM = pl.BlockSpec(memory_space=pltpu.VMEM)
+SMEM = pl.BlockSpec(memory_space=pltpu.SMEM)
+ANY = pl.BlockSpec(memory_space=pl.ANY)
+DMA = pltpu.SemaphoreType.DMA
 
 
 def contract_last(left, right):
     return lax.dot_general(
         left, right, (((1,), (1,)), ((), ())), preferred_element_type=jnp.float32
     )
+
+
+def vmem_out(shape, dtype):
+    return pltpu.VMEM(tuple(shape), dtype)
+
+
+def params(mib):
+    return pltpu.CompilerParams(vmem_limit_bytes=mib << 20)
+
+
+def cost(flops, moved):
+    return pl.CostEstimate(flops=int(flops), bytes_accessed=int(moved), transcendentals=0)
+
+
+def in_hbm(array):
+    return pltpu.with_memory_space_constraint(array, pltpu.HBM)
+
+
+def in_vmem(array):
+    return pltpu.with_memory_space_constraint(array, pltpu.VMEM)
+
+
+def piece_copy(weights, index, piece, sem):
+    return pltpu.make_async_copy(weights.at[pl.ds(index * ROWS, ROWS)], piece, sem)
+
+
+def prefetch_kernel(plan, sources, deps, *refs):
+    weights = refs[:sources]
+    pieces, sems = refs[sources + deps : -1], refs[-1]
+    copies = [
+        piece_copy(weights[which], index, pieces[i], sems.at[i])
+        for i, (which, index) in enumerate(plan)
+    ]
+    for copy in copies:
+        copy.start()
+    for copy in copies:
+        copy.wait()
+
+
+def prefetch(weights, plan, deps):
+    width = weights[0].shape[1]
+    return pl.pallas_call(
+        functools.partial(prefetch_kernel, plan, len(weights), len(deps)),
+        out_shape=[vmem_out((ROWS, width), weights[0].dtype) for _ in plan],
+        in_specs=[HBM] * len(weights) + [ANY] * len(deps),
+        out_specs=[VMEM] * len(plan),
+        scratch_shapes=[DMA((len(plan),))],
+        compiler_params=params(1),
+        cost_estimate=cost(0, len(plan) * ROWS * width * 2),
+        name="prefetch",
+    )(*map(in_hbm, weights), *deps)
+
+
+def attention_kernel(kv_heads, meta, lens, q, nk, nv, k_hbm, v_hbm, wo_hbm, att, wo, kb, vb, rows_f32, sk, sv, sw):
+    count, heads, head = q.shape
+    positions = kb.shape[1]
+    cut = count // CACHE_CUTS
+    copies = []
+    for c in range(CACHE_CUTS):
+        part = pl.ds(c * cut, cut)
+        copies.append(
+            (
+                pltpu.make_async_copy(k_hbm.at[part], kb.at[part], sk.at[c]),
+                pltpu.make_async_copy(v_hbm.at[part], vb.at[part], sv.at[c]),
+            )
+        )
+    fetch = pltpu.make_async_copy(wo_hbm, wo, sw)
+    for pair in copies:
+        for copy in pair:
+            copy.start()
+    fetch.start()
+    base = (meta[0] // kv_heads) * count
+    scale = 1.0 / math.sqrt(head)
+    position = lax.broadcasted_iota(jnp.int32, (heads, positions), 1)
+    for c in range(CACHE_CUTS):
+        for copy in copies[c]:
+            copy.wait()
+        for r in range(c * cut, (c + 1) * cut):
+            query = q[r]
+            score = contract_last(query, kb[r]) * scale
+            score = jnp.where(position < lens[base + r], score, NEG_FILL)
+            own = (
+                jnp.sum(
+                    query.astype(jnp.float32) * nk[r : r + 1].astype(jnp.float32),
+                    axis=1,
+                    keepdims=True,
+                )
+                * scale
+            )
+            top = jnp.maximum(jnp.max(score, axis=1, keepdims=True), own)
+            weight = jnp.exp(score - top)
+            own_weight = jnp.exp(own - top)
+            total = jnp.sum(weight, axis=1, keepdims=True) + own_weight
+            mixed = jnp.dot(
+                weight.astype(jnp.bfloat16), vb[r], preferred_element_type=jnp.float32
+            )
+            own_low = own_weight.astype(jnp.bfloat16).astype(jnp.float32)
+            mixed = mixed + own_low * nv[r : r + 1].astype(jnp.float32)
+            rows_f32[r * heads : (r + 1) * heads, :] = mixed / total
+    for h in range(heads):
+        att[:, h * head : (h + 1) * head] = rows_f32[pl.ds(h, count, stride=heads), :].astype(
+            att.dtype
+        )
+    fetch.wait()
+
+
+def attention(meta, lengths, q, k, v, nk, nv, w_out, kv_heads):
+    count, heads, head = q.shape
+    return pl.pallas_call(
+        functools.partial(attention_kernel, kv_heads),
+        out_shape=[
+            vmem_out((count, heads * head), jnp.bfloat16),
+            vmem_out(w_out.shape, w_out.dtype),
+        ],
+        in_specs=[SMEM, SMEM, VMEM, VMEM, VMEM, HBM, HBM, HBM],
+        out_specs=[VMEM, VMEM],
+        scratch_shapes=[
+            pltpu.VMEM(k.shape, k.dtype),
+            pltpu.VMEM(v.shape, v.dtype),
+            pltpu.VMEM((count * heads, head), jnp.float32),
+            DMA((CACHE_CUTS,)),
+            DMA((CACHE_CUTS,)),
+            DMA,
+        ],
+        compiler_params=params(4),
+        cost_estimate=cost(0, 2 * w_out.size),
+        name="attention",
+    )(meta, lengths, q, nk, nv, in_hbm(k), in_hbm(v), in_hbm(w_out))
+
+
+def stack_kernel(count, *refs):
+    out = refs[-1]
+    for i in range(count):
+        out[i] = refs[i][...]
+
+
+def stack(blocks, deps):
+    return pl.pallas_call(
+        functools.partial(stack_kernel, len(blocks)),
+        out_shape=vmem_out((len(blocks),) + blocks[0].shape, blocks[0].dtype),
+        in_specs=[VMEM] * len(blocks) + [ANY] * len(deps),
+        out_specs=VMEM,
+        compiler_params=params(1),
+        name="stack",
+    )(*blocks, *deps)
+
+
+def swap(value, size, bit):
+    return lax.ppermute(value, "wide", [(i, i ^ bit) for i in range(size)])
+
+
+def shift(value, size, step):
+    return lax.ppermute(value, "wide", [(i, (i + step) % size) for i in range(size)])
+
+
+def place(meta):
+    mine = meta[0]
+    return mine // 4, (mine // 2) % 2, mine % 2
+
+
+def project_kernel(
+    planes, kv_heads, plan, sources, deps, meta, b0, b1, c0, c1, wo, residual, rows_row, gain, *refs
+):
+    weights = refs[:sources]
+    refs = refs[sources + deps :]
+    pieces = refs[: len(plan)]
+    state_ref, message, gathered, sems = refs[len(plan) :]
+    copies = [
+        piece_copy(weights[which], index, pieces[i], sems.at[i])
+        for i, (which, index) in enumerate(plan)
+    ]
+    for copy in copies:
+        copy.start()
+    z, y, core = place(meta)
+    count, width = b0.shape[1:]
+    for block, yy, cc in ((b0, y, core), (c0, y, 1 - core), (b1, 1 - y, core), (c1, 1 - y, 1 - core)):
+        for k in range(planes):
+            source = lax.rem(z + planes - k, planes) * 4 + yy * 2 + cc
+            row = pl.multiple_of((source // kv_heads) * count, count)
+            lane = pl.multiple_of(lax.rem(source, kv_heads) * width, width)
+            gathered[pl.ds(row, count), pl.ds(lane, width)] = block[k]
+    requests, features = residual.shape
+    numbers = lax.broadcasted_iota(jnp.int32, (requests, requests), 0)
+    pick = (rows_row[...] == numbers).astype(jnp.bfloat16)
+    squares = jnp.zeros((requests, 1), jnp.float32)
+    for j in range(0, features, LANES * 2):
+        cut = slice(j, min(j + LANES * 2, features))
+        part = lax.dot_general(
+            pick, residual[:, cut], (((0,), (0,)), ((), ())), preferred_element_type=jnp.float32
+        )
+        part = part + contract_last(gathered[...], wo[cut, :])
+        state_ref[:, cut] = part
+        message[:, cut] = (part * gain[:, cut]).astype(message.dtype)
+        squares = squares + jnp.sum(part * part, axis=1, keepdims=True)
+    high = squares.astype(jnp.bfloat16).astype(jnp.float32)
+    low = squares - high
+    lane = lax.broadcasted_iota(jnp.int32, (requests, LANES), 1)
+    tail = jnp.where(lane == 0, high, jnp.where(lane == 1, low, 0.0))
+    message[:, features:] = tail.astype(message.dtype)
+    for copy in copies:
+        copy.wait()
+
+
+def project(meta, blocks, wo, residual, rows_row, gain, weights, plan, deps, planes, kv_heads):
+    requests, features = residual.shape
+    width = wo.shape[1]
+    return pl.pallas_call(
+        functools.partial(project_kernel, planes, kv_heads, plan, len(weights), len(deps)),
+        out_shape=[vmem_out((ROWS, width), wo.dtype) for _ in plan]
+        + [
+            vmem_out((requests, features), jnp.float32),
+            vmem_out((requests, features + LANES), jnp.bfloat16),
+        ],
+        in_specs=[SMEM] + [VMEM] * 8 + [HBM] * len(weights) + [ANY] * len(deps),
+        out_specs=[VMEM] * (len(plan) + 2),
+        scratch_shapes=[pltpu.VMEM((requests, width), jnp.bfloat16), DMA((max(len(plan), 1),))],
+        compiler_params=params(4),
+        cost_estimate=cost(0, wo.size * 2),
+        name="project",
+    )(meta, *blocks, in_vmem(wo), residual, rows_row, gain, *map(in_hbm, weights), *deps)
+
+
+def half_inputs(z, core, planes, features, block, other, half):
+    for k in range(planes):
+        source = lax.rem(z + planes - k, planes)
+        for part, cc in ((block, core), (other, 1 - core)):
+            lane = pl.multiple_of((source * 2 + cc) * features, features)
+            half[:, pl.ds(lane, features)] = part[k, :, :features]
+
+
+def half_product(half, piece, planes, pair, yy):
+    total = None
+    for zz in range(planes):
+        lane = pl.multiple_of((zz * 2 + yy) * pair, pair)
+        term = contract_last(half[:, zz * pair : (zz + 1) * pair], piece[:, pl.ds(lane, pair)])
+        total = term if total is None else total + term
+    return total
+
+
+def late_copies(weights, first, planes, pair, yy, late, sems):
+    rows = pl.ds(first * ROWS, late.shape[0])
+    copies = []
+    for zz in range(planes):
+        lane = pl.multiple_of((zz * 2 + yy) * pair, pair)
+        copies.append(
+            pltpu.make_async_copy(
+                weights.at[rows, pl.ds(lane, pair)],
+                late.at[:, pl.ds(zz * pair, pair)],
+                sems.at[zz],
+            )
+        )
+    return copies
+
+
+def down_steps(planes):
+    return [(dy, k) for dy in (1, 0) for k in range(planes)]
+
+
+def down_copy(w_down, step, planes, z, y, pair, piece, sem):
+    dy, k = down_steps(planes)[step]
+    yy = 1 - y if dy else y
+    lane = pl.multiple_of((lax.rem(z + k, planes) * 2 + yy) * pair, pair)
+    return pltpu.make_async_copy(w_down.at[:, pl.ds(lane, pair)], piece, sem)
+
+
+def first_half_kernel(planes, count, ready, meta, b0, c0, *refs):
+    gates = refs[:count]
+    ups = refs[count : count + ready]
+    w_up, w_down = refs[count + ready : count + ready + 2]
+    refs = refs[count + ready + 2 :]
+    downs = refs[:DOWN_AHEAD]
+    gate_sum, up_sum, half, late, late_sems, down_sems = refs[DOWN_AHEAD:]
+    z, y, core = place(meta)
+    features = b0.shape[2] - LANES
+    pair = 2 * features
+    copies = late_copies(w_up, ready, planes, pair, y, late, late_sems)
+    ahead = [
+        down_copy(w_down, i, planes, z, y, pair, downs[i], down_sems.at[i])
+        for i in range(DOWN_AHEAD)
+    ]
+    for copy in copies + ahead:
+        copy.start()
+    half_inputs(z, core, planes, features, b0, c0, half)
+    for j in range(count):
+        gate_sum[:, j * ROWS : (j + 1) * ROWS] = half_product(half, gates[j], planes, pair, y)
+    for j in range(ready):
+        up_sum[:, j * ROWS : (j + 1) * ROWS] = half_product(half, ups[j], planes, pair, y)
+    for copy in copies:
+        copy.wait()
+    for j in range(ready, count):
+        rows = slice((j - ready) * ROWS, (j - ready + 1) * ROWS)
+        up_sum[:, j * ROWS : (j + 1) * ROWS] = contract_last(half[...], late[rows, :])
+    for copy in ahead:
+        copy.wait()
+
+
+def first_half(meta, b0, c0, gates, ups, w_up, w_down, planes):
+    count, ready = len(gates), len(ups)
+    requests = b0.shape[1]
+    units, width = w_up.shape
+    pair = 2 * (b0.shape[2] - LANES)
+    return pl.pallas_call(
+        functools.partial(first_half_kernel, planes, count, ready),
+        out_shape=[vmem_out((units, pair), w_down.dtype) for _ in range(DOWN_AHEAD)]
+        + [vmem_out((requests, units), jnp.float32)] * 2,
+        in_specs=[SMEM] + [VMEM] * (2 + count + ready) + [HBM] * 2,
+        out_specs=[VMEM] * (DOWN_AHEAD + 2),
+        scratch_shapes=[
+            pltpu.VMEM((requests, width // 2), jnp.bfloat16),
+            pltpu.VMEM(((count - ready) * ROWS, width // 2), jnp.bfloat16),
+            DMA((planes,)),
+            DMA((DOWN_AHEAD,)),
+        ],
+        compiler_params=params(8),
+        cost_estimate=cost(0, units * width * 2),
+        name="first_half",
+    )(meta, b0, c0, *map(in_vmem, gates), *map(in_vmem, ups), in_hbm(w_up), in_hbm(w_down))
+
+
+def second_half_kernel(
+    planes, count, ready, total_features, meta, b0, c0, b1, c1, gate_sum, up_sum, *refs
+):
+    gates, ups = refs[:count], refs[count : count + ready]
+    downs = refs[count + ready : count + ready + DOWN_AHEAD]
+    refs = refs[count + ready + DOWN_AHEAD :]
+    w_up, w_down, keep, send, half, late, hidden, pieces, result, late_sems, down_sems = refs
+    z, y, core = place(meta)
+    features = b0.shape[2] - LANES
+    pair = 2 * features
+    order = down_steps(planes)
+
+    def fetch(step):
+        slot = step % DOWN_SLOTS
+        return down_copy(w_down, step, planes, z, y, pair, pieces.at[slot], down_sems.at[slot])
+
+    copies = late_copies(w_up, ready, planes, pair, 1 - y, late, late_sems)
+    for copy in copies:
+        copy.start()
+    for step in range(DOWN_AHEAD, min(DOWN_AHEAD + DOWN_SLOTS, len(order))):
+        fetch(step).start()
+    squares = None
+    for block in (b0, c0, b1, c1):
+        for k in range(planes):
+            term = block[k, :, features:].astype(jnp.float32)
+            squares = term if squares is None else squares + term
+    squares = jnp.sum(squares, axis=1, keepdims=True)
+    inv_rms = lax.rsqrt(squares / total_features + EPSILON)
+    half_inputs(z, core, planes, features, b1, c1, half)
+    for j in range(count):
+        cut = slice(j * ROWS, (j + 1) * ROWS)
+        gate = gate_sum[:, cut] + half_product(half, gates[j], planes, pair, 1 - y)
+        if j < ready:
+            up = half_product(half, ups[j], planes, pair, 1 - y)
+        else:
+            if j == ready:
+                for copy in copies:
+                    copy.wait()
+            up = contract_last(half[...], late[(j - ready) * ROWS : (j - ready + 1) * ROWS, :])
+        up = (up_sum[:, cut] + up) * inv_rms
+        gate = gate * inv_rms
+        hidden[:, cut] = (gate * jax.nn.sigmoid(gate) * up).astype(hidden.dtype)
+    mine = pl.ds(pl.multiple_of(core * features, features), features)
+    other = pl.ds(pl.multiple_of((1 - core) * features, features), features)
+    for step, (dy, k) in enumerate(order):
+        spot = dy * planes + k
+        if step < DOWN_AHEAD:
+            piece = downs[step]
+        else:
+            fetch(step).wait()
+            piece = pieces.at[step % DOWN_SLOTS]
+        result[step % 2] = jnp.dot(hidden[...], piece[...], preferred_element_type=jnp.float32)
+        keep[spot] = result[step % 2, :, mine]
+        send[spot] = result[step % 2, :, other].astype(send.dtype)
+        if step >= DOWN_AHEAD and step + DOWN_SLOTS < len(order):
+            fetch(step + DOWN_SLOTS).start()
+
+
+def second_half(meta, blocks, gate_sum, up_sum, gates, ups, downs, w_up, w_down, planes):
+    count, ready = len(gates), len(ups)
+    requests, units = gate_sum.shape
+    width = w_down.shape[1]
+    features = blocks[0].shape[2] - LANES
+    return pl.pallas_call(
+        functools.partial(second_half_kernel, planes, count, ready, width),
+        out_shape=[
+            vmem_out((2 * planes, requests, features), jnp.float32),
+            vmem_out((2 * planes, requests, features), jnp.bfloat16),
+        ],
+        in_specs=[SMEM] + [VMEM] * (6 + count + ready + DOWN_AHEAD) + [HBM] * 2,
+        out_specs=[VMEM] * 2,
+        scratch_shapes=[
+            pltpu.VMEM((requests, width // 2), jnp.bfloat16),
+            pltpu.VMEM(((count - ready) * ROWS, width // 2), jnp.bfloat16),
+            pltpu.VMEM((requests, units), jnp.bfloat16),
+            pltpu.VMEM((DOWN_SLOTS, units, 2 * features), w_down.dtype),
+            pltpu.VMEM((2, requests, 2 * features), jnp.float32),
+            DMA((planes,)),
+            DMA((DOWN_SLOTS,)),
+        ],
+        compiler_params=params(8 + (5 * DOWN_SLOTS + 1) // 2),
+        cost_estimate=cost(0, 2 * units * width * 2),
+        name="second_half",
+    )(
+        meta, *blocks, gate_sum, up_sum, *map(in_vmem, gates), *map(in_vmem, ups),
+        *map(in_vmem, downs), in_hbm(w_up), in_hbm(w_down),
+    )
+
+
+def add_core_kernel(planes, keep, got, stay, send):
+    for k in range(planes):
+        send[k] = (keep[planes + k] + got[planes + k].astype(jnp.float32)).astype(send.dtype)
+        stay[k] = keep[k] + got[k].astype(jnp.float32)
+
+
+def add_core(keep, got, planes):
+    shape = keep.shape[1:]
+    return pl.pallas_call(
+        functools.partial(add_core_kernel, planes),
+        out_shape=[
+            vmem_out((planes,) + shape, jnp.float32),
+            vmem_out((planes,) + shape, jnp.bfloat16),
+        ],
+        in_specs=[VMEM] * 2,
+        out_specs=[VMEM] * 2,
+        compiler_params=params(2),
+        name="add_core",
+    )(keep, got)
+
+
+def add_row_kernel(planes, stay, got, *outs):
+    outs[0][...] = stay[0] + got[0].astype(jnp.float32)
+    for k in range(1, planes):
+        outs[k][...] = (stay[k] + got[k].astype(jnp.float32)).astype(outs[k].dtype)
+
+
+def add_row(stay, got, planes):
+    shape = stay.shape[1:]
+    return pl.pallas_call(
+        functools.partial(add_row_kernel, planes),
+        out_shape=[vmem_out(shape, jnp.float32)]
+        + [vmem_out(shape, jnp.bfloat16) for _ in range(planes - 1)],
+        in_specs=[VMEM] * 2,
+        out_specs=[VMEM] * planes,
+        compiler_params=params(2),
+        name="add_row",
+    )(stay, got)
+
+
+def finish_kernel(state, rows_row, mine, *refs):
+    out = refs[-1]
+    total = state[...] + mine[...]
+    for got in refs[:-1]:
+        total = total + got[...].astype(jnp.float32)
+    requests = total.shape[0]
+    numbers = lax.broadcasted_iota(jnp.int32, (requests, requests), 0)
+    pick = (rows_row[...] == numbers).astype(jnp.bfloat16)
+    out[...] = jnp.dot(
+        pick, total.astype(jnp.bfloat16), preferred_element_type=jnp.float32
+    ).astype(out.dtype)
+
+
+def finish(state, rows_row, mine, got):
+    return pl.pallas_call(
+        finish_kernel,
+        out_shape=jax.ShapeDtypeStruct(state.shape, jnp.bfloat16),
+        in_specs=[VMEM] * (3 + len(got)),
+        out_specs=VMEM,
+        compiler_params=params(2),
+        name="finish",
+    )(state, rows_row, mine, *got)
+
+
+def gather(message, size, planes, first_fill, second_fill):
+    shifted = [shift(message, size, 4 * k) for k in range(1, planes)]
+    fills = first_fill(message)
+    b0 = stack([message] + shifted, fills)
+    b1 = swap(b0, size, 2)
+    c0 = swap(b0, size, 1)
+    between = second_fill(b0, c0)
+    c1 = swap(b1, size, 1)
+    return b0, c0, b1, c1, fills, between
+
+
+def on_device(size, *args):
+    return layer_on_device(size, *args)
+
+
+def layer_on_device(size, queries, keys_cache, values_cache, new_keys, new_values, lengths, assignment,
+              residual, w_out, w_gate, w_up, w_down, norm_gain):
+    planes = size // 4
+    kv_heads = w_out.shape[1] // (queries.shape[2] * queries.shape[3])
+    count = w_gate.shape[0] // ROWS
+    meta = lax.axis_index("wide").astype(jnp.int32).reshape(1)
+    requests = assignment.shape[0]
+    att, wo = attention(
+        meta, lengths, queries[0], keys_cache[0], values_cache[0], new_keys[0], new_values[0],
+        w_out, kv_heads,
+    )
+    order = [(0, j) for j in range(count)] + [(1, j) for j in range(count)]
+    ready = 2
+    early = order[: count + ready]
+    plans = [early[0:1], early[1:3], early[3:4], early[4:6], early[6:7]]
+    weights = (w_gate, w_up)
+    pieces = []
+
+    b0, c0, b1, c1, f0, f1 = gather(
+        att, size, planes,
+        lambda m: prefetch(weights, plans[0], [m]),
+        lambda b, c: prefetch(weights, plans[1], [b]),
+    )
+    f2 = prefetch(weights, plans[2], [b1, f1[0]])
+    outs = project(
+        meta, (b0, b1, c0, c1), wo, residual, assignment.reshape(1, requests),
+        norm_gain.reshape(1, -1), weights, plans[3], [f2[0]], planes, kv_heads,
+    )
+    f3, (state, message) = outs[: len(plans[3])], outs[len(plans[3]) :]
+    pieces = list(f0) + list(f1) + list(f2) + list(f3)
+
+    def second_fill(b, c):
+        return first_half(
+            meta, b, c, pieces[:count], pieces[count:], w_up, w_down, planes
+        )
+
+    def first_fill(m):
+        got = prefetch(weights, plans[4], [m])
+        pieces.extend(got)
+        return got
+
+    b0, c0, b1, c1, _, outs = gather(message, size, planes, first_fill, second_fill)
+    downs, (gate_sum, up_sum) = outs[:-2], outs[-2:]
+    keep, send = second_half(
+        meta, (b0, c0, b1, c1), gate_sum, up_sum, pieces[:count], pieces[count:], downs,
+        w_up, w_down, planes,
+    )
+    stay, send = add_core(keep, swap(send, size, 1), planes)
+    parts = add_row(stay, swap(send, size, 2), planes)
+    got = [shift(parts[k], size, 4 * k) for k in range(1, planes)]
+    return finish(state, assignment.reshape(1, requests), parts[0], got)
 
 
 def masked_scores(query_rows, keys_local, lens_local, block_index, inv_scale):
@@ -30,7 +579,7 @@
     return jnp.where(position < lens_local[:, None, None], scores, NEG_FILL)
 
 
-def on_device(
+def plain_on_device(
     queries,
     keys_cache,
     values_cache,
@@ -45,8 +594,9 @@
     w_down,
     norm_gain,
 ):
+    kv_heads = w_out.shape[1] // (queries.shape[2] * queries.shape[3])
     my_index = lax.axis_index("wide")
-    my_shard = my_index // KV
+    my_shard = my_index // kv_heads
     req_dev = queries.shape[1]
     query_rows = queries[0]
     keys_local = keys_cache[0]
@@ -93,8 +643,8 @@
     head_piece = lax.all_gather(attended, "wide", axis=0, tiled=True)
 
     def one_source(offset, running):
-        source_shard = offset // KV
-        source_group = offset % KV
+        source_shard = offset // kv_heads
+        source_group = offset % kv_heads
         request_ids = lax.dynamic_slice_in_dim(assignment, source_shard * req_dev, req_dev)
         out_cols = lax.dynamic_slice_in_dim(w_out, source_group * feat_width, feat_width, 1)
         source_rows = lax.dynamic_index_in_dim(head_piece, offset, 0, keepdims=False)
@@ -109,7 +659,7 @@
     )
     hidden_state = residual.astype(jnp.float32) + projected
     row_squares = lax.psum(jnp.sum(hidden_state * hidden_state, axis=1), "wide")
-    inv_rms = lax.rsqrt(row_squares / D + EPSILON)
+    inv_rms = lax.rsqrt(row_squares / w_out.shape[1] + EPSILON)
     normed_cols = (hidden_state * inv_rms[:, None] * norm_gain[None, :]).astype(jnp.bfloat16)
     normed_piece = lax.all_gather(normed_cols, "wide", axis=1, tiled=True)
     gate_val = contract_last(normed_piece, w_gate)
@@ -120,7 +670,20 @@
     return (hidden_state + down_part).astype(jnp.bfloat16)
 
 
+def fits(size, w_out, w_gate):
+    features, units = w_out.shape[0] // size, w_gate.shape[0] // size
+    resident = 2 * units * w_gate.shape[1] * 2
+    return (
+        size % 4 == 0
+        and features % LANES == 0
+        and units % ROWS == 0
+        and units // ROWS >= 5
+        and resident <= 44 << 20
+    )
+
+
 def solution(mesh):
+    size = mesh.shape["wide"]
     placed = (
         P(("groups", "wide"), None, None, None),
         P(("groups", "wide"), None, None, None),
@@ -136,6 +699,16 @@
         P("wide", None),
         P("wide"),
     )
-    return jax.shard_map(
-        on_device, mesh=mesh, in_specs=placed, out_specs=P("groups", "wide"), check_vma=False
-    )
+
+    def sharded(body):
+        return jax.shard_map(
+            body, mesh=mesh, in_specs=placed, out_specs=P("groups", "wide"), check_vma=False
+        )
+
+    fast = sharded(functools.partial(on_device, size))
+    plain = sharded(plain_on_device)
+
+    def layer(*args):
+        return (fast if fits(size, args[8], args[9]) else plain)(*args)
+
+    return layer

time: 250 us -> 93.4 us (0.37)
  matrix products: 77.6 us -> 0 us
  blocking collectives: 70.1 us -> 0 us
  Pallas kernels: 0 us -> 49.7 us
  waiting for transfers between devices: 56.4 us -> 18.8 us
  other arithmetic: 29.4 us -> 0 us
  starting transfers between devices: 0.01 us -> 19.3 us
  between operations: 14.2 us -> 0.21 us
  local copies, waits for them, and re-layouts: 0.04 us -> 4.99 us
    dot_general x35 -> x0, matrix products: 77.6 us -> none  [the longest x18 46.5 us: contract_last(): lax.dot_general(left, right, (((1,), (1,)), ((), ())), preferred_element_...]
    reduce_scatter x1 -> x0, waiting for transfers between devices: 56.4 us -> none  [on_device(): lax.psum_scatter(down_terms, 'wide', scatter_dimension=1, tiled=True)]
    pallas_call x0 -> x13, Pallas kernels: none -> 49.7 us  [the longest x1 17.4 us: second_half(): pl.pallas_call(functools.partial(second_half_kernel, planes, count, ready...]
    all_gather x2 -> x0, blocking collectives: 40.3 us -> none  [the longest x1 21.5 us: on_device(): head_piece = lax.all_gather(attended, 'wide', axis=0, tiled=True)]
    psum x1 -> x0, blocking collectives: 29.8 us -> none  [on_device(): row_squares = lax.psum(jnp.sum(hidden_state * hidden_state, axis=1), 'wide')]
    ppermute x0 -> x17, starting transfers between devices: none -> 19.3 us  [the longest x9 14 us: shift(): lax.ppermute(value, 'wide', [(i, (i + step) % size) for i in range(size)])]
    ppermute x0 -> x17, waiting for transfers between devices: none -> 18.8 us  [the longest x8 12.7 us: swap(): return lax.ppermute(value, 'wide', [(i, i ^ bit) for i in range(size)])]
    scatter-add x16 -> x0, other arithmetic: 12 us -> none  [one_source(): return running.at[request_ids].add(term)]
  transfers between devices with their start and end apart: 1 -> 17, of which waited for: 1 -> 10; matrix products, arithmetic and copies ran while one was open for 0% -> 0% of each run, Pallas kernels for 0% -> 23%
where the time goes in v1:
time: 93.4 us; the launch traced here: 93 us
  Pallas kernels  49.7 us (53%)
  starting transfers between devices  19.3 us (21%)
  waiting for transfers between devices  18.8 us (20%)
  local copies, waits for them, and re-layouts  4.99 us (5%)
    pallas_call x1, Pallas kernels, second_half(): pl.pallas_call(functools.partial(second_half_kernel, planes, count, ready...  17.4 us
    ppermute x9, starting transfers between devices, shift(): lax.ppermute(value, 'wide', [(i, (i + step) % size) for i in range(size)])  14 us
    ppermute x8, waiting for transfers between devices, swap(): return lax.ppermute(value, 'wide', [(i, i ^ bit) for i in range(size)])  12.7 us
    pallas_call x4, Pallas kernels, prefetch(): pl.pallas_call(functools.partial(prefetch_kernel, plan, len(weights), len...  11.6 us
    pallas_call x1, Pallas kernels, first_half(): pl.pallas_call(functools.partial(first_half_kernel, planes, count, ready)...  10.2 us
    ppermute x9, waiting for transfers between devices, shift(): lax.ppermute(value, 'wide', [(i, (i + step) % size) for i in range(size)])  6.11 us
    pallas_call x1, Pallas kernels, attention(): pl.pallas_call(functools.partial(attention_kernel, kv_heads), out_shape=[...  5.98 us
    ppermute x8, starting transfers between devices, swap(): return lax.ppermute(value, 'wide', [(i, i ^ bit) for i in range(size)])  5.32 us
  transfers between devices with their start and end apart: 17, of which 10 were waited for; matrix products, arithmetic and copies ran while one was open for 0% of the time, Pallas kernels for 23%

profile of v1, /device:TPU:0, one launch (start us, length us, event | category | flops | bytes accessed | tf_op | source)
XLA Modules:
  0.0 93.0 jit_solution(4400347964652081370)
XLA Ops:
  0.0 0.0 copy-start.2
  0.0 0.8 copy-done.2
  0.8 0.0 copy-start.4
  0.8 0.7 copy-done.4
  1.4 0.0 copy-start.5
  1.4 0.7 copy-done.5
  2.1 0.0 copy-start.8
  2.1 0.7 copy-done.8
  2.8 6.0 %attention.1 = (bf16[16,1024]{1,0:T(8,128)(2,1)S(1)}, bf16[512,8192]{1,0:T(8,128)(2,1)S(1)}) custom-call(s32[1]{0:T(128)} %bitcast.meta, s32[32]{0:T(128)S(1)} %copy-done.8, bf16[16,8,128]{2,1,0:T(8,128)(2,1)S(1)} %bitcast.8, bf16[16,128]{1,0:T(8,128)(2,1)S(1)} %bitcast.9, bf16[16,128]{1,0:T(8,128)(2,1)S(1)} %bitcast.10, bf16[16,320,128]{2,1,0:T(8,128)(2,1)} %bitcast.14, ...), custom_call_target="tpu_custom_call" | custom-call | bytes 8388608 | tf_op jit(solution)/shard_map/attention/pallas_call | solution.py:140
  8.8 5.1 %collective-permute-start.2 = (bf16[16,1024]{1,0:T(8,128)(2,1)S(1)}, bf16[16,1024]{1,0:T(8,128)(2,1)S(1)}, u32[]{:S(2)}, u32[]{:S(2)}) collective-permute-start(bf16[16,1024]{1,0:T(8,128)(2,1)S(1)} %get-tuple-element.25.refs_2_.refs_0_), channel_id=1, source_target_pairs={{0,12},{1,13},{2,14},{3,15},{4,0},{5,1},{6,2},{7,3},{8,4},{9,5},{1... | collective-permute-start | bytes 98312 | tf_op jit(solution)/shard_map/ppermute | solution.py:184
  13.9 0.0 collective-permute-start.1
  13.9 1.0 %collective-permute-start = (bf16[16,1024]{1,0:T(8,128)(2,1)S(1)}, bf16[16,1024]{1,0:T(8,128)(2,1)S(1)}, u32[]{:S(2)}, u32[]{:S(2)}) collective-permute-start(bf16[16,1024]{1,0:T(8,128)(2,1)S(1)} %get-tuple-element.25.refs_2_.refs_0_), channel_id=1, source_target_pairs={{0,4},{1,5},{2,6},{3,7},{4,8},{5,9},{6,10},{7,11},{8,12},{9,13},{1... | collective-permute-start | bytes 98312 | tf_op jit(solution)/shard_map/ppermute | solution.py:184
  14.9 2.2 %prefetch.4.refs_4_.refs_0_ = bf16[256,8192]{1,0:T(8,128)(2,1)S(1)} custom-call(bf16[1280,8192]{1,0:T(8,128)(2,1)} %refs_0_.9, bf16[1280,8192]{1,0:T(8,128)(2,1)} %refs_9_.1, bf16[16,1024]{1,0:T(8,128)(2,1)S(1)} %get-tuple-element.25.refs_2_.refs_0_), custom_call_target="tpu_custom_call" | custom-call | bytes 4194304 | tf_op jit(solution)/shard_map/prefetch/pallas_call | solution.py:73
  17.1 0.0 collective-permute-done.2.refs_3_
  17.1 1.6 %collective-permute-done.1.refs_2_ = bf16[16,1024]{1,0:T(8,128)(2,1)S(1)} collective-permute-done((bf16[16,1024]{1,0:T(8,128)(2,1)S(1)}, bf16[16,1024]{1,0:T(8,128)(2,1)S(1)}, u32[]{:S(2)}, u32[]{:S(2)}) %collective-permute-start.1) | collective-permute-done | bytes 32800 | tf_op jit(solution)/shard_map/ppermute | solution.py:184
  18.7 0.9 collective-permute-done.refs_1_
  19.6 1.6 %collective-permute-start.3 = (bf16[4,16,1024]{2,1,0:T(8,128)(2,1)S(1)}, bf16[4,16,1024]{2,1,0:T(8,128)(2,1)S(1)}, u32[]{:S(2)}, u32[]{:S(2)}) collective-permute-start(bf16[4,16,1024]{2,1,0:T(8,128)(2,1)S(1)} %stack.2.refs_2_.b0), channel_id=1, source_target_pairs={{0,2},{1,3},{2,0},{3,1},{4,6},{5,7},{6,4},{7,5},{8,10},{9,11},{10,... | collective-permute-start | bytes 393224 | tf_op jit(solution)/shard_map/ppermute | solution.py:180
  21.2 0.0 collective-permute-start.4
  21.2 3.4 %collective-permute-done.3.refs_2_.b1 = bf16[4,16,1024]{2,1,0:T(8,128)(2,1)S(1)} collective-permute-done((bf16[4,16,1024]{2,1,0:T(8,128)(2,1)S(1)}, bf16[4,16,1024]{2,1,0:T(8,128)(2,1)S(1)}, u32[]{:S(2)}, u32[]{:S(2)}) %collective-permute-start.3) | collective-permute-done | bytes 131104 | tf_op jit(solution)/shard_map/ppermute | solution.py:180
  24.7 0.0 collective-permute-start.5
  24.7 3.5 %prefetch.5 = (bf16[256,8192]{1,0:T(8,128)(2,1)S(1)}, bf16[256,8192]{1,0:T(8,128)(2,1)S(1)}) custom-call(bf16[1280,8192]{1,0:T(8,128)(2,1)} %refs_0_.9, bf16[1280,8192]{1,0:T(8,128)(2,1)} %refs_9_.1, bf16[4,16,1024]{2,1,0:T(8,128)(2,1)S(1)} %stack.2.refs_2_.b0), custom_call_target="tpu_custom_call" | custom-call | bytes 8388608 | tf_op jit(solution)/shard_map/prefetch/pallas_call | solution.py:73
  28.2 0.0 copy-start
  28.2 0.0 copy-start.3
  28.2 0.0 copy-start.6
  28.2 0.0 copy-start.7
  28.2 3.7 %prefetch.6.refs_2_.refs_3_ = bf16[256,8192]{1,0:T(8,128)(2,1)S(1)} custom-call(bf16[1280,8192]{1,0:T(8,128)(2,1)} %refs_0_.9, bf16[1280,8192]{1,0:T(8,128)(2,1)} %refs_9_.1, bf16[4,16,1024]{2,1,0:T(8,128)(2,1)S(1)} %collective-permute-done.3.refs_2_.b1, bf16[256,8192]{1,0:T(8,128)(2,1)S(1)} %get-tuple-element.27.refs_3_.refs_1_), custom_call_target="tpu_custom_call" | custom-call | bytes 4194304 | tf_op jit(solution)/shard_map/prefetch/pallas_call | solution.py:73
  31.9 0.0 collective-permute-done.4.c0
  32.0 0.0 collective-permute-done.5.c1
  32.0 0.0 copy-done.3
  32.0 0.0 copy-done.6
  32.0 0.0 copy-done.7
  32.0 3.6 %project.1 = (bf16[256,8192]{1,0:T(8,128)(2,1)S(1)}, bf16[256,8192]{1,0:T(8,128)(2,1)S(1)}, f32[32,512]{1,0:T(8,128)S(1)}, bf16[32,640]{1,0:T(8,128)(2,1)S(1)}) custom-call(s32[1]{0:T(128)} %bitcast.meta, bf16[4,16,1024]{2,1,0:T(8,128)(2,1)S(1)} %stack.2.refs_2_.b0, bf16[4,16,1024]{2,1,0:T(8,128)(2,1)S(1)} %collective-permute-done.3.refs_2_.b1, ...), custom_call_target="tpu_custom_call" | custom-call | bytes 8388608 | tf_op jit(solution)/shard_map/project/pallas_call | solution.py:238
  35.6 0.6 collective-permute-start.8
  36.3 0.9 collective-permute-start.7
  37.2 1.7 %collective-permute-start.6 = (bf16[32,640]{1,0:T(8,128)(2,1)S(1)}, bf16[32,640]{1,0:T(8,128)(2,1)S(1)}, u32[]{:S(2)}, u32[]{:S(2)}) collective-permute-start(bf16[32,640]{1,0:T(8,128)(2,1)S(1)} %get-tuple-element.29.refs_2_.refs_0_), channel_id=1, source_target_pairs={{0,4},{1,5},{2,6},{3,7},{4,8},{5,9},{6,10},{7,11},{8,12},{9,13},{1... | collective-permute-start | bytes 122888 | tf_op jit(solution)/shard_map/ppermute | solution.py:184
  38.8 2.2 %prefetch.7.refs_4_.refs_6_ = bf16[256,8192]{1,0:T(8,128)(2,1)S(1)} custom-call(bf16[1280,8192]{1,0:T(8,128)(2,1)} %refs_0_.9, bf16[1280,8192]{1,0:T(8,128)(2,1)} %refs_9_.1, bf16[32,640]{1,0:T(8,128)(2,1)S(1)} %get-tuple-element.29.refs_2_.refs_0_), custom_call_target="tpu_custom_call" | custom-call | bytes 4194304 | tf_op jit(solution)/shard_map/prefetch/pallas_call | solution.py:73
  41.0 0.0 collective-permute-done.8.refs_3_
  41.1 1.4 %collective-permute-done.7.refs_2_ = bf16[32,640]{1,0:T(8,128)(2,1)S(1)} collective-permute-done((bf16[32,640]{1,0:T(8,128)(2,1)S(1)}, bf16[32,640]{1,0:T(8,128)(2,1)S(1)}, u32[]{:S(2)}, u32[]{:S(2)}) %collective-permute-start.7) | collective-permute-done | bytes 40992 | tf_op jit(solution)/shard_map/ppermute | solution.py:184
  42.5 0.5 collective-permute-done.6.refs_1_
  43.0 1.6 %collective-permute-start.10 = (bf16[4,32,640]{2,1,0:T(8,128)(2,1)S(1)}, bf16[4,32,640]{2,1,0:T(8,128)(2,1)S(1)}, u32[]{:S(2)}, u32[]{:S(2)}) collective-permute-start(bf16[4,32,640]{2,1,0:T(8,128)(2,1)S(1)} %stack.3.b0), channel_id=1, source_target_pairs={{0,2},{1,3},{2,0},{3,1},{4,6},{5,7},{6,4},{7,5},{8,10},{9,11},{10,... | collective-permute-start | bytes 491528 | tf_op jit(solution)/shard_map/ppermute | solution.py:180
  44.6 0.0 collective-permute-start.9
  44.6 3.8 %collective-permute-done.10.b1 = bf16[4,32,640]{2,1,0:T(8,128)(2,1)S(1)} collective-permute-done((bf16[4,32,640]{2,1,0:T(8,128)(2,1)S(1)}, bf16[4,32,640]{2,1,0:T(8,128)(2,1)S(1)}, u32[]{:S(2)}, u32[]{:S(2)}) %collective-permute-start.10) | collective-permute-done | bytes 163872 | tf_op jit(solution)/shard_map/ppermute | solution.py:180
  48.4 0.0 collective-permute-start.11
  48.4 0.0 collective-permute-done.9.c0
  48.4 0.0 copy-done
  48.4 10.2 %first_half.1 = (bf16[1280,1024]{1,0:T(8,128)(2,1)S(1)}, bf16[1280,1024]{1,0:T(8,128)(2,1)S(1)}, f32[32,1280]{1,0:T(8,128)S(1)}, f32[32,1280]{1,0:T(8,128)S(1)}) custom-call(s32[1]{0:T(128)} %bitcast.meta, bf16[4,32,640]{2,1,0:T(8,128)(2,1)S(1)} %stack.3.b0, bf16[4,32,640]{2,1,0:T(8,128)(2,1)S(1)} %collective-permute-done.9.c0, ...), custom_call_target="tpu_custom_call" | custom-call | bytes 20971520 | tf_op jit(solution)/shard_map/first_half/pallas_call | solution.py:333
  58.6 0.0 collective-permute-done.11.c1
  58.6 0.0 copy-start.1
  58.6 2.2 %copy-done.1 = bf16[256,8192]{1,0:T(8,128)(2,1)S(1)} copy-done((bf16[256,8192]{1,0:T(8,128)(2,1)S(1)}, bf16[256,8192]{1,0:T(8,128)(2,1)}, u32[]{:S(2)}) %copy-start.1) | copy-done | bytes 4194328
  60.8 17.4 %second_half.1 = (f32[8,32,512]{2,1,0:T(8,128)S(1)}, bf16[8,32,512]{2,1,0:T(8,128)(2,1)S(1)}) custom-call(s32[1]{0:T(128)} %bitcast.meta, bf16[4,32,640]{2,1,0:T(8,128)(2,1)S(1)} %stack.3.b0, bf16[4,32,640]{2,1,0:T(8,128)(2,1)S(1)} %collective-permute-done.9.c0, bf16[4,32,640]{2,1,0:T(8,128)(2,1)S(1)} %collective-permute-done.10.b1, ...), custom_call_target="tpu_custom_call" | custom-call | bytes 41943040 | tf_op jit(solution)/shard_map/second_half/pallas_call | solution.py:414
  78.2 0.6 collective-permute-start.12
  78.8 1.2 %collective-permute-done.12.got = bf16[8,32,512]{2,1,0:T(8,128)(2,1)S(1)} collective-permute-done((bf16[8,32,512]{2,1,0:T(8,128)(2,1)S(1)}, bf16[8,32,512]{2,1,0:T(8,128)(2,1)S(1)}, u32[]{:S(2)}, u32[]{:S(2)}) %collective-permute-start.12) | collective-permute-done | bytes 262176 | tf_op jit(solution)/shard_map/ppermute | solution.py:180
  80.0 0.1 add_core.1
  80.0 1.6 %collective-permute-start.13 = (bf16[4,32,512]{2,1,0:T(8,128)(2,1)S(1)}, bf16[4,32,512]{2,1,0:T(8,128)(2,1)S(1)}, u32[]{:S(2)}, u32[]{:S(2)}) collective-permute-start(bf16[4,32,512]{2,1,0:T(8,128)(2,1)S(1)} %get-tuple-element.40), channel_id=1, source_target_pairs={{0,2},{1,3},{2,0},{3,1},{4,6},{5,7},{6,4},{7,5},{8,10},{9,11},{10,... | collective-permute-start | bytes 393224 | tf_op jit(solution)/shard_map/ppermute | solution.py:180
  81.6 4.3 %collective-permute-done.13.got = bf16[4,32,512]{2,1,0:T(8,128)(2,1)S(1)} collective-permute-done((bf16[4,32,512]{2,1,0:T(8,128)(2,1)S(1)}, bf16[4,32,512]{2,1,0:T(8,128)(2,1)S(1)}, u32[]{:S(2)}, u32[]{:S(2)}) %collective-permute-start.13) | collective-permute-done | bytes 131104 | tf_op jit(solution)/shard_map/ppermute | solution.py:180
  85.9 0.1 collective-permute-start.14
  85.9 2.2 %collective-permute-start.15 = (bf16[32,512]{1,0:T(8,128)(2,1)S(1)}, bf16[32,512]{1,0:T(8,128)(2,1)S(1)}, u32[]{:S(2)}, u32[]{:S(2)}) collective-permute-start(bf16[32,512]{1,0:T(8,128)(2,1)S(1)} %get-tuple-element.43), channel_id=1, source_target_pairs={{0,8},{1,9},{2,10},{3,11},{4,12},{5,13},{6,14},{7,15},{8,0},{9,1},... | collective-permute-start | bytes 98312 | tf_op jit(solution)/shard_map/ppermute | solution.py:184
  88.2 2.3 %collective-permute-start.16 = (bf16[32,512]{1,0:T(8,128)(2,1)S(1)}, bf16[32,512]{1,0:T(8,128)(2,1)S(1)}, u32[]{:S(2)}, u32[]{:S(2)}) collective-permute-start(bf16[32,512]{1,0:T(8,128)(2,1)S(1)} %get-tuple-element.44), channel_id=1, source_target_pairs={{0,12},{1,13},{2,14},{3,15},{4,0},{5,1},{6,2},{7,3},{8,4},{9,5},{1... | collective-permute-start | bytes 98312 | tf_op jit(solution)/shard_map/ppermute | solution.py:184
  90.5 1.2 %collective-permute-done.14.refs_0_ = bf16[32,512]{1,0:T(8,128)(2,1)S(1)} collective-permute-done((bf16[32,512]{1,0:T(8,128)(2,1)S(1)}, bf16[32,512]{1,0:T(8,128)(2,1)S(1)}, u32[]{:S(2)}, u32[]{:S(2)}) %collective-permute-start.14) | collective-permute-done | bytes 32800 | tf_op jit(solution)/shard_map/ppermute | solution.py:184
  91.7 0.0 collective-permute-done.15.refs_1_
  91.7 0.5 collective-permute-done.16.refs_2_
  92.2 0.8 finish.1
  (3 shorter events, 0.0 us)
Async XLA Ops:
  0.0 0.8 copy-start.2
  0.8 0.7 copy-start.4
  1.4 0.7 copy-start.5
  2.1 0.7 copy-start.8
  8.8 8.4 %collective-permute-start.2 = (bf16[16,1024]{1,0:T(8,128)(2,1)S(1)}, bf16[16,1024]{1,0:T(8,128)(2,1)S(1)}, u32[]{:S(2)}, u32[]{:S(2)}) collective-permute-start(bf16[16,1024]{1,0:T(8,128)(2,1)S(1)} %get-tuple-element.25.refs_2_.refs_0_), channel_id=1, source_target_pairs={{0,12},{1,13},{2,14},{3,15},{4,0},{5,1},{6,2},{7,3},{8,4},{9,5},{1... | collective-permute-start | bytes 98312 | tf_op jit(solution)/shard_map/ppermute | solution.py:184
  13.9 4.8 %collective-permute-start.1 = (bf16[16,1024]{1,0:T(8,128)(2,1)S(1)}, bf16[16,1024]{1,0:T(8,128)(2,1)S(1)}, u32[]{:S(2)}, u32[]{:S(2)}) collective-permute-start(bf16[16,1024]{1,0:T(8,128)(2,1)S(1)} %get-tuple-element.25.refs_2_.refs_0_), channel_id=1, source_target_pairs={{0,8},{1,9},{2,10},{3,11},{4,12},{5,13},{6,14},{7,15},{8,0},{9,1},... | collective-permute-start | bytes 98312 | tf_op jit(solution)/shard_map/ppermute | solution.py:184
  13.9 5.7 %collective-permute-start = (bf16[16,1024]{1,0:T(8,128)(2,1)S(1)}, bf16[16,1024]{1,0:T(8,128)(2,1)S(1)}, u32[]{:S(2)}, u32[]{:S(2)}) collective-permute-start(bf16[16,1024]{1,0:T(8,128)(2,1)S(1)} %get-tuple-element.25.refs_2_.refs_0_), channel_id=1, source_target_pairs={{0,4},{1,5},{2,6},{3,7},{4,8},{5,9},{6,10},{7,11},{8,12},{9,13},{1... | collective-permute-start | bytes 98312 | tf_op jit(solution)/shard_map/ppermute | solution.py:184
  19.6 5.0 %collective-permute-start.3 = (bf16[4,16,1024]{2,1,0:T(8,128)(2,1)S(1)}, bf16[4,16,1024]{2,1,0:T(8,128)(2,1)S(1)}, u32[]{:S(2)}, u32[]{:S(2)}) collective-permute-start(bf16[4,16,1024]{2,1,0:T(8,128)(2,1)S(1)} %stack.2.refs_2_.b0), channel_id=1, source_target_pairs={{0,2},{1,3},{2,0},{3,1},{4,6},{5,7},{6,4},{7,5},{8,10},{9,11},{10,... | collective-permute-start | bytes 393224 | tf_op jit(solution)/shard_map/ppermute | solution.py:180
  21.2 10.7 %collective-permute-start.4 = (bf16[4,16,1024]{2,1,0:T(8,128)(2,1)S(1)}, bf16[4,16,1024]{2,1,0:T(8,128)(2,1)S(1)}, u32[]{:S(2)}, u32[]{:S(2)}) collective-permute-start(bf16[4,16,1024]{2,1,0:T(8,128)(2,1)S(1)} %stack.2.refs_2_.b0), channel_id=1, source_target_pairs={{0,1},{1,0},{2,3},{3,2},{4,5},{5,4},{6,7},{7,6},{8,9},{9,8},{10,11... | collective-permute-start | bytes 393224 | tf_op jit(solution)/shard_map/ppermute | solution.py:180
  24.7 7.3 %collective-permute-start.5 = (bf16[4,16,1024]{2,1,0:T(8,128)(2,1)S(1)}, bf16[4,16,1024]{2,1,0:T(8,128)(2,1)S(1)}, u32[]{:S(2)}, u32[]{:S(2)}) collective-permute-start(bf16[4,16,1024]{2,1,0:T(8,128)(2,1)S(1)} %collective-permute-done.3.refs_2_.b1), channel_id=1, source_target_pairs={{0,1},{1,0},{2,3},{3,2},{4,5},{5,4},{6,7},{7,6},{8,9},{9,8},{10,11... | collective-permute-start | bytes 393224 | tf_op jit(solution)/shard_map/ppermute | solution.py:180
  28.2 20.2 %copy-start = (bf16[256,8192]{1,0:T(8,128)(2,1)}, bf16[256,8192]{1,0:T(8,128)(2,1)S(1)}, u32[]{:S(2)}) copy-start(bf16[256,8192]{1,0:T(8,128)(2,1)S(1)} %get-tuple-element.30.refs_2_) | copy-start | bytes 12582916
  28.2 3.8 %copy-start.3 = (bf16[32,512]{1,0:T(8,128)(2,1)S(1)}, bf16[32,512]{1,0:T(8,128)(2,1)}, u32[]{:S(2)}) copy-start(bf16[32,512]{1,0:T(8,128)(2,1)} %residual.1) | copy-start | bytes 98308
  28.2 3.8 %copy-start.6 = (f32[512]{0:T(512)S(1)}, f32[512]{0:T(512)}, u32[]{:S(2)}) copy-start(f32[512]{0:T(512)} %param.25) | copy-start | bytes 6148
  28.2 3.8 %copy-start.7 = (s32[32]{0:T(128)S(1)}, s32[32]{0:T(128)}, u32[]{:S(2)}) copy-start(s32[32]{0:T(128)} %param.19) | copy-start | bytes 388
  35.6 5.4 %collective-permute-start.8 = (bf16[32,640]{1,0:T(8,128)(2,1)S(1)}, bf16[32,640]{1,0:T(8,128)(2,1)S(1)}, u32[]{:S(2)}, u32[]{:S(2)}) collective-permute-start(bf16[32,640]{1,0:T(8,128)(2,1)S(1)} %get-tuple-element.29.refs_2_.refs_0_), channel_id=1, source_target_pairs={{0,12},{1,13},{2,14},{3,15},{4,0},{5,1},{6,2},{7,3},{8,4},{9,5},{1... | collective-permute-start | bytes 122888 | tf_op jit(solution)/shard_map/ppermute | solution.py:184
  36.3 6.2 %collective-permute-start.7 = (bf16[32,640]{1,0:T(8,128)(2,1)S(1)}, bf16[32,640]{1,0:T(8,128)(2,1)S(1)}, u32[]{:S(2)}, u32[]{:S(2)}) collective-permute-start(bf16[32,640]{1,0:T(8,128)(2,1)S(1)} %get-tuple-element.29.refs_2_.refs_0_), channel_id=1, source_target_pairs={{0,8},{1,9},{2,10},{3,11},{4,12},{5,13},{6,14},{7,15},{8,0},{9,1},... | collective-permute-start | bytes 122888 | tf_op jit(solution)/shard_map/ppermute | solution.py:184
  37.2 5.8 %collective-permute-start.6 = (bf16[32,640]{1,0:T(8,128)(2,1)S(1)}, bf16[32,640]{1,0:T(8,128)(2,1)S(1)}, u32[]{:S(2)}, u32[]{:S(2)}) collective-permute-start(bf16[32,640]{1,0:T(8,128)(2,1)S(1)} %get-tuple-element.29.refs_2_.refs_0_), channel_id=1, source_target_pairs={{0,4},{1,5},{2,6},{3,7},{4,8},{5,9},{6,10},{7,11},{8,12},{9,13},{1... | collective-permute-start | bytes 122888 | tf_op jit(solution)/shard_map/ppermute | solution.py:184
  43.0 5.4 %collective-permute-start.10 = (bf16[4,32,640]{2,1,0:T(8,128)(2,1)S(1)}, bf16[4,32,640]{2,1,0:T(8,128)(2,1)S(1)}, u32[]{:S(2)}, u32[]{:S(2)}) collective-permute-start(bf16[4,32,640]{2,1,0:T(8,128)(2,1)S(1)} %stack.3.b0), channel_id=1, source_target_pairs={{0,2},{1,3},{2,0},{3,1},{4,6},{5,7},{6,4},{7,5},{8,10},{9,11},{10,... | collective-permute-start | bytes 491528 | tf_op jit(solution)/shard_map/ppermute | solution.py:180
  44.6 3.8 %collective-permute-start.9 = (bf16[4,32,640]{2,1,0:T(8,128)(2,1)S(1)}, bf16[4,32,640]{2,1,0:T(8,128)(2,1)S(1)}, u32[]{:S(2)}, u32[]{:S(2)}) collective-permute-start(bf16[4,32,640]{2,1,0:T(8,128)(2,1)S(1)} %stack.3.b0), channel_id=1, source_target_pairs={{0,1},{1,0},{2,3},{3,2},{4,5},{5,4},{6,7},{7,6},{8,9},{9,8},{10,11... | collective-permute-start | bytes 491528 | tf_op jit(solution)/shard_map/ppermute | solution.py:180
  48.4 10.2 %collective-permute-start.11 = (bf16[4,32,640]{2,1,0:T(8,128)(2,1)S(1)}, bf16[4,32,640]{2,1,0:T(8,128)(2,1)S(1)}, u32[]{:S(2)}, u32[]{:S(2)}) collective-permute-start(bf16[4,32,640]{2,1,0:T(8,128)(2,1)S(1)} %collective-permute-done.10.b1), channel_id=1, source_target_pairs={{0,1},{1,0},{2,3},{3,2},{4,5},{5,4},{6,7},{7,6},{8,9},{9,8},{10,11... | collective-permute-start | bytes 491528 | tf_op jit(solution)/shard_map/ppermute | solution.py:180
  58.6 2.2 %copy-start.1 = (bf16[256,8192]{1,0:T(8,128)(2,1)S(1)}, bf16[256,8192]{1,0:T(8,128)(2,1)}, u32[]{:S(2)}) copy-start(bf16[256,8192]{1,0:T(8,128)(2,1)} %copy-done) | copy-start | bytes 12582916
  78.2 1.7 %collective-permute-start.12 = (bf16[8,32,512]{2,1,0:T(8,128)(2,1)S(1)}, bf16[8,32,512]{2,1,0:T(8,128)(2,1)S(1)}, u32[]{:S(2)}, u32[]{:S(2)}) collective-permute-start(bf16[8,32,512]{2,1,0:T(8,128)(2,1)S(1)} %get-tuple-element.38), channel_id=1, source_target_pairs={{0,1},{1,0},{2,3},{3,2},{4,5},{5,4},{6,7},{7,6},{8,9},{9,8},{10,11... | collective-permute-start | bytes 786440 | tf_op jit(solution)/shard_map/ppermute | solution.py:180
  80.0 5.8 %collective-permute-start.13 = (bf16[4,32,512]{2,1,0:T(8,128)(2,1)S(1)}, bf16[4,32,512]{2,1,0:T(8,128)(2,1)S(1)}, u32[]{:S(2)}, u32[]{:S(2)}) collective-permute-start(bf16[4,32,512]{2,1,0:T(8,128)(2,1)S(1)} %get-tuple-element.40), channel_id=1, source_target_pairs={{0,2},{1,3},{2,0},{3,1},{4,6},{5,7},{6,4},{7,5},{8,10},{9,11},{10,... | collective-permute-start | bytes 393224 | tf_op jit(solution)/shard_map/ppermute | solution.py:180
  85.9 5.8 %collective-permute-start.14 = (bf16[32,512]{1,0:T(8,128)(2,1)S(1)}, bf16[32,512]{1,0:T(8,128)(2,1)S(1)}, u32[]{:S(2)}, u32[]{:S(2)}) collective-permute-start(bf16[32,512]{1,0:T(8,128)(2,1)S(1)} %get-tuple-element.42), channel_id=1, source_target_pairs={{0,4},{1,5},{2,6},{3,7},{4,8},{5,9},{6,10},{7,11},{8,12},{9,13},{1... | collective-permute-start | bytes 98312 | tf_op jit(solution)/shard_map/ppermute | solution.py:184
  85.9 5.7 %collective-permute-start.15 = (bf16[32,512]{1,0:T(8,128)(2,1)S(1)}, bf16[32,512]{1,0:T(8,128)(2,1)S(1)}, u32[]{:S(2)}, u32[]{:S(2)}) collective-permute-start(bf16[32,512]{1,0:T(8,128)(2,1)S(1)} %get-tuple-element.43), channel_id=1, source_target_pairs={{0,8},{1,9},{2,10},{3,11},{4,12},{5,13},{6,14},{7,15},{8,0},{9,1},... | collective-permute-start | bytes 98312 | tf_op jit(solution)/shard_map/ppermute | solution.py:184
  88.2 4.0 %collective-permute-start.16 = (bf16[32,512]{1,0:T(8,128)(2,1)S(1)}, bf16[32,512]{1,0:T(8,128)(2,1)S(1)}, u32[]{:S(2)}, u32[]{:S(2)}) collective-permute-start(bf16[32,512]{1,0:T(8,128)(2,1)S(1)} %get-tuple-element.44), channel_id=1, source_target_pairs={{0,12},{1,13},{2,14},{3,15},{4,0},{5,1},{6,2},{7,3},{8,4},{9,5},{1... | collective-permute-start | bytes 98312 | tf_op jit(solution)/shard_map/ppermute | solution.py:184
